TPU v7x, 256 devices: a whole 4x4x8 slice. The times are simulated.
256 devices in a mesh: sub: 64 (over x, z, core), blk: 4 (over y).
Axes of the slice: x: 4, y: 4, z: 8, core: 2. Of those that a mesh axis runs over, the one named last changes fastest.
Arguments:
- residual: float32 [64, 8, 375, 256], P('sub', 'blk'), may hold values from -6 to 6
- stiffness: bfloat16 [64, 8, 16, 375, 375], P('sub', 'blk'), may hold values from -0.078125 to 0.078125
- pattern: int32 [64, 8, 16], P('sub', 'blk'), may hold values from 0 to 7
- neumann_inv: bfloat16 [64, 8, 375, 375], P('sub', 'blk'), may hold values from -0.3125 to 0.3125
- dirichlet_inv: bfloat16 [64, 8, 375, 375], P('sub', 'blk'), may hold values from -0.3125 to 0.3125
- basis: bfloat16 [64, 8, 375, 192], P('sub', 'blk'), may hold values from -0.5 to 0.5
- node_ops: float32 [64, 6, 192, 192], P('sub'), as said below
- root_inv: float32 [192, 192], replicated, may hold values from -0.4375 to 0.4375
Outputs:
- preconditioned: float32 [64, 8, 375, 256], P('sub', 'blk')
Inputs may be any that keep to these rules, and one draw needn't show every extreme that they name: node_ops[s, l] equals node_ops[t, l] whenever s // 2**l == t // 2**l: one map for each tree node, held by all of its subdomains.
All inputs are finite; a program needn't handle non-finite values.
Results may differ from a plain program's by a relative error of at most 0.004.
Values may be sent and summed in bfloat16 or wider, within the bound.
A program may use at most 64 MiB of HBM per device.

v0:
```python
import jax
import jax.numpy as jnp
from jax import lax
from jax.sharding import PartitionSpec as P


def swapped(x, axis, distance):
    return lax.ppermute(x, axis, [(i, i ^ 1 << distance) for i in range(lax.axis_size(axis))])


def passed_along(x, axis, by):
    count = lax.axis_size(axis)
    pairs = [(i, i + by) for i in range(count) if 0 <= i + by < count]
    return lax.ppermute(x, axis, pairs)


def tree_solve(values, maps, root_inv):
    highest = lax.Precision.HIGHEST
    level_values = [values]
    current = values
    for level in range(maps.shape[0]):
        own = jnp.einsum("mk,mr->kr", maps[level], current, precision=highest)
        current = own + swapped(own, "sub", level)
        level_values.append(current)
    field = jnp.dot(root_inv, current, precision=highest)
    for level in reversed(range(maps.shape[0])):
        field = jnp.dot(maps[level], field, precision=highest) + level_values[level]
    return field


def shards(residual, stiffness, pattern, neumann_inv, dirichlet_inv, basis, node_ops, root_inv):
    subs = lax.axis_size("sub")
    here = lax.axis_index("sub")
    per_device = residual.shape[1]
    local_ids = jnp.arange(per_device)
    shared = (local_ids == 0) & (here > 0) | (local_ids == per_device - 1) & (here < subs - 1)
    scale = jnp.where(shared, 0.5, 1.0).astype(jnp.float32)[:, None, None]
    scaled_bf = (residual[0] * scale).astype(jnp.bfloat16)
    local_fix = jnp.einsum(
        "jab,jbr->jar", neumann_inv[0], scaled_bf, preferred_element_type=jnp.float32
    )
    partial_coarse = jnp.einsum(
        "jbm,jbr->mr", basis[0], scaled_bf, preferred_element_type=jnp.float32
    )
    total = lax.psum(partial_coarse, "blk")
    coarse_fix = tree_solve(total, node_ops[0], root_inv).astype(jnp.bfloat16)
    fix_term = jnp.einsum("jbm,mr->jbr", basis[0], coarse_fix, preferred_element_type=jnp.float32)
    combined = ((local_fix + fix_term) * scale)[None]
    incoming = passed_along(combined[:, -1], "sub", 1)
    first = combined[:, 0] + incoming
    returned = passed_along(first, "sub", -1)
    last = jnp.where(here < subs - 1, returned, combined[:, -1])
    assembled = jnp.concatenate([first[:, None], combined[:, 1:-1], last[:, None]], axis=1)
    assembled_bf = assembled.astype(jnp.bfloat16)
    gathered = lax.all_gather(assembled_bf, "blk", axis=1, tiled=True)
    picked = jnp.take(gathered[0], pattern[0], axis=0)
    coupled = jnp.einsum("jpab,jpbr->jar", stiffness[0], picked, preferred_element_type=jnp.float32)
    correction = jnp.einsum(
        "jab,jbr->jar",
        dirichlet_inv[0],
        coupled.astype(jnp.bfloat16),
        preferred_element_type=jnp.float32,
    )
    result = assembled[0] - jnp.where(shared[:, None, None], 0.0, correction)
    return result[None]


def solution(mesh):
    placed = (
        P("sub", "blk", None, None),
        P("sub", "blk", None, None, None),
        P("sub", "blk", None),
        P("sub", "blk", None, None),
        P("sub", "blk", None, None),
        P("sub", "blk", None, None),
        P("sub", None, None, None),
        P(),
    )
    return jax.shard_map(
        shards, mesh=mesh, in_specs=placed, out_specs=P("sub", "blk", None, None), check_vma=False
    )
```

profile of v0, /device:TPU:1, one launch (start us, length us, event | category | flops | bytes accessed | tf_op | source)
XLA Modules:
  0.0 188.2 jit_solution(13424925944676565091)
XLA Ops:
  6.6 2.3 %convolution_bitcast_fusion.14 = f32[192,256]{1,0:T(8,128)} fusion(bf16[1,2,375,192]{2,3,1,0:T(8,128)(2,1)} %param.13, f32[1,2,375,256]{3,1,2,0:T(2,128)} %param.8, f32[2]{0:T(128)S(1)} %get-tuple-element.5), kind=kOutput, calls=%fused_computation.31 | convolution fusion | flops 74112000 | bytes 1252616 | tf_op jit(solution)/shard_map/jbm,jbr->mr/dot_general | solution.py:42
  8.9 0.0 all-reduce.2.cloned.1.call-update
  8.9 0.0 all-gather.2.cloned.1.call-start
  8.9 49.2 %all-reduce.2.cloned.1.call-done = f32[192,256]{1,0:T(8,128)} async-done(((f32[192,256]{1,0:T(8,128)}), f32[192,256]{1,0:T(8,128)}) %all-reduce.2.cloned.1.call-update) | async-done | bytes 196624 | tf_op jit(solution)/shard_map/psum | solution.py:45
  58.2 1.5 convolution_bitcast_fusion.13
  59.7 2.9 %collective-permute-start = (f32[192,256]{1,0:T(8,128)S(1)}, f32[192,256]{1,0:T(8,128)S(1)}, u32[]{:S(2)}, u32[]{:S(2)}) collective-permute-start(f32[192,256]{1,0:T(8,128)S(1)} %convolution_bitcast_fusion.13), channel_id=1, source_target_pairs={{0,4},{4,0},{8,12},{12,8},{16,20},{20,16},{24,28},{28,24},{32,36},... | collective-permute-start | bytes 589832 | tf_op jit(solution)/shard_map/ppermute | solution.py:8
  62.6 1.1 collective-permute-done
  63.6 0.6 convolution_bitcast_fusion.12
  64.2 1.4 collective-permute-start.1
  65.6 4.8 %collective-permute-done.1 = f32[192,256]{1,0:T(8,128)S(1)} collective-permute-done((f32[192,256]{1,0:T(8,128)S(1)}, f32[192,256]{1,0:T(8,128)S(1)}, u32[]{:S(2)}, u32[]{:S(2)}) %collective-permute-start.1) | collective-permute-done | bytes 196640 | tf_op jit(solution)/shard_map/ppermute | solution.py:8
  70.4 0.6 convolution_bitcast_fusion.11
  71.0 2.3 %collective-permute-start.2 = (f32[192,256]{1,0:T(8,128)S(1)}, f32[192,256]{1,0:T(8,128)S(1)}, u32[]{:S(2)}, u32[]{:S(2)}) collective-permute-start(f32[192,256]{1,0:T(8,128)S(1)} %convolution_bitcast_fusion.11), channel_id=1, source_target_pairs={{0,16},{4,20},{8,24},{12,28},{16,0},{20,4},{24,8},{28,12},{32,48},... | collective-permute-start | bytes 589832 | tf_op jit(solution)/shard_map/ppermute | solution.py:8
  73.4 8.7 %collective-permute-done.2 = f32[192,256]{1,0:T(8,128)S(1)} collective-permute-done((f32[192,256]{1,0:T(8,128)S(1)}, f32[192,256]{1,0:T(8,128)S(1)}, u32[]{:S(2)}, u32[]{:S(2)}) %collective-permute-start.2) | collective-permute-done | bytes 196640 | tf_op jit(solution)/shard_map/ppermute | solution.py:8
  82.1 0.6 convolution_bitcast_fusion.10
  82.7 6.4 %collective-permute-start.3 = (f32[192,256]{1,0:T(8,128)S(1)}, f32[192,256]{1,0:T(8,128)S(1)}, u32[]{:S(2)}, u32[]{:S(2)}) collective-permute-start(f32[192,256]{1,0:T(8,128)S(1)} %convolution_bitcast_fusion.10), channel_id=1, source_target_pairs={{0,32},{4,36},{8,40},{12,44},{16,48},{20,52},{24,56},{28,60},{32,0... | collective-permute-start | bytes 589832 | tf_op jit(solution)/shard_map/ppermute | solution.py:8
  89.1 7.4 %collective-permute-done.3 = f32[192,256]{1,0:T(8,128)S(1)} collective-permute-done((f32[192,256]{1,0:T(8,128)S(1)}, f32[192,256]{1,0:T(8,128)S(1)}, u32[]{:S(2)}, u32[]{:S(2)}) %collective-permute-start.3) | collective-permute-done | bytes 196640 | tf_op jit(solution)/shard_map/ppermute | solution.py:8
  96.6 0.6 convolution_bitcast_fusion.9
  97.2 1.3 collective-permute-start.4
  98.4 3.9 %collective-permute-done.4 = f32[192,256]{1,0:T(8,128)S(1)} collective-permute-done((f32[192,256]{1,0:T(8,128)S(1)}, f32[192,256]{1,0:T(8,128)S(1)}, u32[]{:S(2)}, u32[]{:S(2)}) %collective-permute-start.4) | collective-permute-done | bytes 196640 | tf_op jit(solution)/shard_map/ppermute | solution.py:8
  102.3 0.6 convolution_bitcast_fusion.8
  102.9 2.8 %collective-permute-start.5 = (f32[192,256]{1,0:T(8,128)S(1)}, f32[192,256]{1,0:T(8,128)S(1)}, u32[]{:S(2)}, u32[]{:S(2)}) collective-permute-start(f32[192,256]{1,0:T(8,128)S(1)} %convolution_bitcast_fusion.8), channel_id=1, source_target_pairs={{0,128},{4,132},{8,136},{12,140},{16,144},{20,148},{24,152},{28,15... | collective-permute-start | bytes 589832 | tf_op jit(solution)/shard_map/ppermute | solution.py:8
  105.7 3.3 %collective-permute-done.5 = f32[192,256]{1,0:T(8,128)S(1)} collective-permute-done((f32[192,256]{1,0:T(8,128)S(1)}, f32[192,256]{1,0:T(8,128)S(1)}, u32[]{:S(2)}, u32[]{:S(2)}) %collective-permute-start.5) | collective-permute-done | bytes 196640 | tf_op jit(solution)/shard_map/ppermute | solution.py:8
  109.0 0.3 fusion.52
  109.4 0.3 fusion.23
  109.7 0.3 fusion.22
  110.0 0.3 fusion.21
  110.4 0.3 fusion.20
  110.7 0.3 fusion.19
  111.1 0.3 fusion.25
  111.4 0.3 convolution_bitcast_fusion.1
  111.8 0.1 copy-done.2
  111.9 0.4 fusion.12
  112.3 0.1 fusion.70
  112.4 0.4 copy.61
  112.8 2.7 %collective-permute-start.6 = (f32[1,375,256]{2,0,1:T(1,128)S(1)}, f32[1,375,256]{2,0,1:T(1,128)S(1)}, u32[]{:S(2)}, u32[]{:S(2)}) collective-permute-start(f32[1,375,256]{2,0,1:T(1,128)S(1)} %bitcast.158), channel_id=1, source_target_pairs={{0,4},{4,8},{8,12},{12,16},{16,20},{20,24},{24,28},{28,32},{32,36}... | collective-permute-start | bytes 1152008 | tf_op jit(solution)/shard_map/ppermute | solution.py:14
  115.5 4.6 %collective-permute-done.6 = f32[1,375,256]{2,0,1:T(1,128)S(1)} collective-permute-done((f32[1,375,256]{2,0,1:T(1,128)S(1)}, f32[1,375,256]{2,0,1:T(1,128)S(1)}, u32[]{:S(2)}, u32[]{:S(2)}) %collective-permute-start.6) | collective-permute-done | bytes 384032 | tf_op jit(solution)/shard_map/ppermute | solution.py:14
  120.1 0.5 fusion.36
  120.6 2.1 %collective-permute-start.7 = (f32[1,375,256]{2,0,1:T(1,128)S(1)}, f32[1,375,256]{2,0,1:T(1,128)S(1)}, u32[]{:S(2)}, u32[]{:S(2)}) collective-permute-start(f32[1,375,256]{2,0,1:T(1,128)S(1)} %fusion.36), channel_id=1, source_target_pairs={{4,0},{8,4},{12,8},{16,12},{20,16},{24,20},{28,24},{32,28},{36,32}... | collective-permute-start | bytes 1152008 | tf_op jit(solution)/shard_map/ppermute | solution.py:14
  122.7 7.6 %collective-permute-done.7 = f32[1,375,256]{2,0,1:T(1,128)S(1)} collective-permute-done((f32[1,375,256]{2,0,1:T(1,128)S(1)}, f32[1,375,256]{2,0,1:T(1,128)S(1)}, u32[]{:S(2)}, u32[]{:S(2)}) %collective-permute-start.7) | collective-permute-done | bytes 384032 | tf_op jit(solution)/shard_map/ppermute | solution.py:14
  130.3 0.5 fusion.35
  130.8 0.7 fusion.39
  131.6 0.8 copy.30
  132.3 0.0 all-gather.2.cloned.1.call-update
  132.4 0.1 reshape.96
  132.5 31.0 %all-gather.2.cloned.1.call-done = bf16[1,8,375,256]{3,2,0,1:T(8,128)(2,1)} async-done(((bf16[1,2,375,256]{3,2,0,1:T(8,128)(2,1)}), bf16[1,8,375,256]{3,2,0,1:T(8,128)(2,1)}) %all-gather.2.cloned.1.call-update) | async-done | bytes 1536016 | tf_op jit(solution)/shard_map/all_gather | solution.py:55
  163.5 5.0 %gather_fusion = bf16[32,375,256]{2,1,0:T(8,128)(2,1)} fusion(bf16[8,375,256]{2,1,0:T(8,128)(2,1)} %bitcast.154, s32[1024]{0:T(1024)S(1)} %pad_clamp_fusion), kind=kCustom, calls=%fused_computation | custom fusion | bytes 12288128 | tf_op jit(solution)/shard_map/jit(_take)/gather | solution.py:56
  168.5 11.0 %fusion.28 = f32[2,256,375]{1,2,0:T(8,128)S(1)} fusion(bf16[2,375,375]{2,0,1:T(2,128)(2,1)S(1)} %bitcast.160, bf16[2,16,375,375]{3,1,2,0:T(8,128)(2,1)} %bitcast.159, bf16[2,16,375,256]{3,2,1,0:T(8,128)(2,1)} %bitcast.155, pred[2,16]{1,0:T(4,128)(4,1)S(1)} %compare_and_fusion), kind=kOutput, calls=%fused_computation.41 | convolution fusion | flops 2451264000 | bytes 16474532 | tf_op jit(solution)/shard_map/jab,jbr->jar/dot_general | solution.py:58
  179.6 1.8 fusion.27
  (25 shorter events, 0.2 us)
Async XLA Ops:
  6.5 105.2 %copy-start = (bf16[1,2,375,375]{3,1,2,0:T(2,128)(2,1)S(1)}, bf16[1,2,375,375]{3,1,2,0:T(2,128)(2,1)}, u32[]{:S(2)}) copy-start(bf16[1,2,375,375]{3,1,2,0:T(2,128)(2,1)} %param.11) | copy-start | bytes 1687504
  6.5 51.6 %copy-start.1 = (f32[1,6,192,192]{3,2,1,0:T(8,128)S(1)}, f32[1,6,192,192]{3,2,1,0:T(8,128)}, u32[]{:S(2)}) copy-start(f32[1,6,192,192]{3,2,1,0:T(8,128)} %param.14) | copy-start | bytes 2654212
  6.5 51.6 %all-reduce.2.cloned.1.call-start = ((), (), s32[]{:S(2)}) async-start(), calls=%async_computation | async-start | bytes 393216 | tf_op jit(solution)/shard_map/psum | solution.py:45
  8.9 154.6 %all-gather.2.cloned.1.call-start = ((), (), s32[]{:S(2)}) async-start(), calls=%async_computation.1 | async-start | bytes 1925120 | tf_op jit(solution)/shard_map/all_gather | solution.py:55
  59.7 3.9 %collective-permute-start = (f32[192,256]{1,0:T(8,128)S(1)}, f32[192,256]{1,0:T(8,128)S(1)}, u32[]{:S(2)}, u32[]{:S(2)}) collective-permute-start(f32[192,256]{1,0:T(8,128)S(1)} %convolution_bitcast_fusion.13), channel_id=1, source_target_pairs={{0,4},{4,0},{8,12},{12,8},{16,20},{20,16},{24,28},{28,24},{32,36},... | collective-permute-start | bytes 589832 | tf_op jit(solution)/shard_map/ppermute | solution.py:8
  64.2 6.2 %collective-permute-start.1 = (f32[192,256]{1,0:T(8,128)S(1)}, f32[192,256]{1,0:T(8,128)S(1)}, u32[]{:S(2)}, u32[]{:S(2)}) collective-permute-start(f32[192,256]{1,0:T(8,128)S(1)} %convolution_bitcast_fusion.12), channel_id=1, source_target_pairs={{0,8},{4,12},{8,0},{12,4},{16,24},{20,28},{24,16},{28,20},{32,40},... | collective-permute-start | bytes 589832 | tf_op jit(solution)/shard_map/ppermute | solution.py:8
  71.0 11.0 %collective-permute-start.2 = (f32[192,256]{1,0:T(8,128)S(1)}, f32[192,256]{1,0:T(8,128)S(1)}, u32[]{:S(2)}, u32[]{:S(2)}) collective-permute-start(f32[192,256]{1,0:T(8,128)S(1)} %convolution_bitcast_fusion.11), channel_id=1, source_target_pairs={{0,16},{4,20},{8,24},{12,28},{16,0},{20,4},{24,8},{28,12},{32,48},... | collective-permute-start | bytes 589832 | tf_op jit(solution)/shard_map/ppermute | solution.py:8
  82.7 26.4 %copy-start.5 = (f32[192,192]{1,0:T(8,128)S(1)}, f32[192,192]{1,0:T(8,128)}, u32[]{:S(2)}) copy-start(f32[192,192]{1,0:T(8,128)} %param.15) | copy-start | bytes 442372
  82.7 13.9 %collective-permute-start.3 = (f32[192,256]{1,0:T(8,128)S(1)}, f32[192,256]{1,0:T(8,128)S(1)}, u32[]{:S(2)}, u32[]{:S(2)}) collective-permute-start(f32[192,256]{1,0:T(8,128)S(1)} %convolution_bitcast_fusion.10), channel_id=1, source_target_pairs={{0,32},{4,36},{8,40},{12,44},{16,48},{20,52},{24,56},{28,60},{32,0... | collective-permute-start | bytes 589832 | tf_op jit(solution)/shard_map/ppermute | solution.py:8
  97.2 5.1 %collective-permute-start.4 = (f32[192,256]{1,0:T(8,128)S(1)}, f32[192,256]{1,0:T(8,128)S(1)}, u32[]{:S(2)}, u32[]{:S(2)}) collective-permute-start(f32[192,256]{1,0:T(8,128)S(1)} %convolution_bitcast_fusion.9), channel_id=1, source_target_pairs={{0,64},{4,68},{8,72},{12,76},{16,80},{20,84},{24,88},{28,92},{32,9... | collective-permute-start | bytes 589832 | tf_op jit(solution)/shard_map/ppermute | solution.py:8
  102.9 6.1 %collective-permute-start.5 = (f32[192,256]{1,0:T(8,128)S(1)}, f32[192,256]{1,0:T(8,128)S(1)}, u32[]{:S(2)}, u32[]{:S(2)}) collective-permute-start(f32[192,256]{1,0:T(8,128)S(1)} %convolution_bitcast_fusion.8), channel_id=1, source_target_pairs={{0,128},{4,132},{8,136},{12,140},{16,144},{20,148},{24,152},{28,15... | collective-permute-start | bytes 589832 | tf_op jit(solution)/shard_map/ppermute | solution.py:8
  110.0 1.0 copy-start.4
  110.4 1.0 copy-start.3
  110.7 1.1 copy-start.2
  112.8 7.3 %collective-permute-start.6 = (f32[1,375,256]{2,0,1:T(1,128)S(1)}, f32[1,375,256]{2,0,1:T(1,128)S(1)}, u32[]{:S(2)}, u32[]{:S(2)}) collective-permute-start(f32[1,375,256]{2,0,1:T(1,128)S(1)} %bitcast.158), channel_id=1, source_target_pairs={{0,4},{4,8},{8,12},{12,16},{16,20},{20,24},{24,28},{28,32},{32,36}... | collective-permute-start | bytes 1152008 | tf_op jit(solution)/shard_map/ppermute | solution.py:14
  120.6 9.7 %collective-permute-start.7 = (f32[1,375,256]{2,0,1:T(1,128)S(1)}, f32[1,375,256]{2,0,1:T(1,128)S(1)}, u32[]{:S(2)}, u32[]{:S(2)}) collective-permute-start(f32[1,375,256]{2,0,1:T(1,128)S(1)} %fusion.36), channel_id=1, source_target_pairs={{4,0},{8,4},{12,8},{16,12},{20,16},{24,20},{28,24},{32,28},{36,32}... | collective-permute-start | bytes 1152008 | tf_op jit(solution)/shard_map/ppermute | solution.py:14
  130.8 1.5 copy-start.6
  163.5 5.0 %copy-start.7 = (bf16[1,2,375,375]{3,1,2,0:T(2,128)(2,1)S(1)}, bf16[1,2,375,375]{3,1,2,0:T(2,128)(2,1)}, u32[]{:S(2)}) copy-start(bf16[1,2,375,375]{3,1,2,0:T(2,128)(2,1)} %param.12) | copy-start | bytes 1687504
Sparse Core Ops, SparseCore 0:
  9.7 48.4 all-reduce.1
  132.5 30.9 all-gather.1
where the time goes:
time: 188 us
  waiting for transfers between devices  122 us (65%)
  starting transfers between devices  21.9 us (12%)
  matrix products  20.8 us (11%)
  between operations  13.6 us (7%)
  local copies, waits for them, and re-layouts  6.44 us (3%)
  other arithmetic  3.71 us (2%)
    psum x1, waiting for transfers between devices, shards(): total = lax.psum(partial_coarse, 'blk')  49.2 us
    all_gather x1, waiting for transfers between devices, shards(): gathered = lax.all_gather(assembled_bf, 'blk', axis=1, tiled=True)  31 us
    ppermute x6, waiting for transfers between devices, swapped(): lax.ppermute(x, axis, [(i, i ^ 1 << distance) for i in range(lax.axis_siz...  29.2 us
    ppermute x6, starting transfers between devices, swapped(): lax.ppermute(x, axis, [(i, i ^ 1 << distance) for i in range(lax.axis_siz...  17.1 us
    ppermute x2, waiting for transfers between devices, passed_along(): return lax.ppermute(x, axis, pairs)  12.2 us
    dot_general x1, matrix products, shards(): jnp.einsum('jab,jbr->jar', dirichlet_inv[0], coupled.astype(jnp.bfloat16)...  11 us
    gather x1, local copies, waits for them, and re-layouts, shards(): picked = jnp.take(gathered[0], pattern[0], axis=0)  5.01 us
    ppermute x2, starting transfers between devices, passed_along(): return lax.ppermute(x, axis, pairs)  4.79 us
  transfers between devices with their start and end apart: 10, of which 10 were waited for; matrix products, arithmetic and copies ran while one was open for 0% of the time, Pallas kernels for 0%

commit v1 on v0

--- a/solution.py
+++ b/solution.py
@@ -2,6 +2,15 @@
 import jax.numpy as jnp
 from jax import lax
 from jax.sharding import PartitionSpec as P
+
+
+def doubling_sum(x, axis):
+    size = lax.axis_size(axis)
+    summed, reach = (x, 1)
+    while reach < size:
+        summed = summed + lax.ppermute(summed, axis, [(i, i ^ reach) for i in range(size)])
+        reach = 2 * reach
+    return summed
 
 
 def swapped(x, axis, distance):
@@ -42,7 +51,7 @@
     partial_coarse = jnp.einsum(
         "jbm,jbr->mr", basis[0], scaled_bf, preferred_element_type=jnp.float32
     )
-    total = lax.psum(partial_coarse, "blk")
+    total = doubling_sum(partial_coarse, "blk")
     coarse_fix = tree_solve(total, node_ops[0], root_inv).astype(jnp.bfloat16)
     fix_term = jnp.einsum("jbm,mr->jbr", basis[0], coarse_fix, preferred_element_type=jnp.float32)
     combined = ((local_fix + fix_term) * scale)[None]

time: 188 us -> 159 us (0.85)
  waiting for transfers between devices: 122 us -> 79.6 us
  starting transfers between devices: 21.9 us -> 30.3 us
  matrix products: 20.8 us -> 24.8 us
    psum x1 -> x0, waiting for transfers between devices: 49.2 us -> none  [shards(): total = lax.psum(partial_coarse, 'blk')]
    ppermute x0 -> x2, waiting for transfers between devices: none -> 6.51 us  [doubling_sum(): lax.ppermute(summed, axis, [(i, i ^ reach) for i in range(size)])]
    ppermute x0 -> x2, starting transfers between devices: none -> 6.24 us  [doubling_sum(): lax.ppermute(summed, axis, [(i, i ^ reach) for i in range(size)])]
    dot_general x6, matrix products: 4.43 us -> 9.17 us  [tree_solve(): own = jnp.einsum('mk,mr->kr', maps[level], current, precision=highest)]
  transfers between devices with their start and end apart: 10 -> 11, of which waited for: 10 -> 11; matrix products, arithmetic and copies ran while one was open for 0% -> 0% of each run, Pallas kernels for 0% -> 0%
where the time goes in v1:
time: 159 us
  waiting for transfers between devices  79.6 us (50%)
  starting transfers between devices  30.3 us (19%)
  matrix products  24.8 us (16%)
  between operations  13.6 us (9%)
  local copies, waits for them, and re-layouts  6.46 us (4%)
  other arithmetic  3.76 us (2%)
    all_gather x1, waiting for transfers between devices, shards(): gathered = lax.all_gather(assembled_bf, 'blk', axis=1, tiled=True)  32 us
    ppermute x6, waiting for transfers between devices, swapped(): lax.ppermute(x, axis, [(i, i ^ 1 << distance) for i in range(lax.axis_siz...  28.9 us
    ppermute x6, starting transfers between devices, swapped(): lax.ppermute(x, axis, [(i, i ^ 1 << distance) for i in range(lax.axis_siz...  18.2 us
    ppermute x2, waiting for transfers between devices, passed_along(): return lax.ppermute(x, axis, pairs)  12.2 us
    dot_general x1, matrix products, shards(): jnp.einsum('jab,jbr->jar', dirichlet_inv[0], coupled.astype(jnp.bfloat16)...  11 us
    dot_general x6, matrix products, tree_solve(): own = jnp.einsum('mk,mr->kr', maps[level], current, precision=highest)  9.17 us
    ppermute x2, waiting for transfers between devices, doubling_sum(): lax.ppermute(summed, axis, [(i, i ^ reach) for i in range(size)])  6.51 us
    ppermute x2, starting transfers between devices, doubling_sum(): lax.ppermute(summed, axis, [(i, i ^ reach) for i in range(size)])  6.24 us
  transfers between devices with their start and end apart: 11, of which 11 were waited for; matrix products, arithmetic and copies ran while one was open for 0% of the time, Pallas kernels for 0%

profile of v1, /device:TPU:1, one launch (start us, length us, event | category | flops | bytes accessed | tf_op | source)
XLA Modules:
  0.0 158.7 jit_solution(10859131019039054373)
XLA Ops:
  6.5 1.6 convolution_bitcast_fusion.14
  8.1 2.2 %collective-permute-start = (f32[192,256]{1,0:T(8,128)S(1)}, f32[192,256]{1,0:T(8,128)S(1)}, u32[]{:S(2)}, u32[]{:S(2)}) collective-permute-start(f32[192,256]{1,0:T(8,128)S(1)} %convolution_bitcast_fusion.14), channel_id=1, source_target_pairs={{0,1},{1,0},{2,3},{3,2},{4,5},{5,4},{6,7},{7,6},{8,9},{9,8},{10,11... | collective-permute-start | bytes 589832 | tf_op jit(solution)/shard_map/ppermute | solution.py:11
  10.3 3.4 %collective-permute-done = f32[192,256]{1,0:T(8,128)S(1)} collective-permute-done((f32[192,256]{1,0:T(8,128)S(1)}, f32[192,256]{1,0:T(8,128)S(1)}, u32[]{:S(2)}, u32[]{:S(2)}) %collective-permute-start) | collective-permute-done | bytes 196640 | tf_op jit(solution)/shard_map/ppermute | solution.py:11
  13.8 4.0 %collective-permute-start.1 = (f32[192,256]{1,0:T(8,128)S(1)}, f32[192,256]{1,0:T(8,128)S(1)}, u32[]{:S(2)}, u32[]{:S(2)}) collective-permute-start(f32[192,256]{1,0:T(8,128)S(1)} %add.69), channel_id=1, source_target_pairs={{0,2},{1,3},{2,0},{3,1},{4,6},{5,7},{6,4},{7,5},{8,10},{9,11},{10,... | collective-permute-start | bytes 589832 | tf_op jit(solution)/shard_map/ppermute | solution.py:11
  17.8 3.1 %collective-permute-done.1 = f32[192,256]{1,0:T(8,128)S(1)} collective-permute-done((f32[192,256]{1,0:T(8,128)S(1)}, f32[192,256]{1,0:T(8,128)S(1)}, u32[]{:S(2)}, u32[]{:S(2)}) %collective-permute-start.1) | collective-permute-done | bytes 196640 | tf_op jit(solution)/shard_map/ppermute | solution.py:11
  20.9 1.5 convolution_bitcast_fusion.13
  22.4 3.6 %collective-permute-start.2 = (f32[192,256]{1,0:T(8,128)S(1)}, f32[192,256]{1,0:T(8,128)S(1)}, u32[]{:S(2)}, u32[]{:S(2)}) collective-permute-start(f32[192,256]{1,0:T(8,128)S(1)} %convolution_bitcast_fusion.13), channel_id=1, source_target_pairs={{0,4},{4,0},{8,12},{12,8},{16,20},{20,16},{24,28},{28,24},{32,36},... | collective-permute-start | bytes 589832 | tf_op jit(solution)/shard_map/ppermute | solution.py:17
  26.0 1.1 collective-permute-done.2
  27.1 1.5 convolution_bitcast_fusion.12
  28.6 1.1 collective-permute-start.3
  29.7 5.1 %collective-permute-done.3 = f32[192,256]{1,0:T(8,128)S(1)} collective-permute-done((f32[192,256]{1,0:T(8,128)S(1)}, f32[192,256]{1,0:T(8,128)S(1)}, u32[]{:S(2)}, u32[]{:S(2)}) %collective-permute-start.3) | collective-permute-done | bytes 196640 | tf_op jit(solution)/shard_map/ppermute | solution.py:17
  34.8 1.5 convolution_bitcast_fusion.11
  36.3 2.8 %collective-permute-start.4 = (f32[192,256]{1,0:T(8,128)S(1)}, f32[192,256]{1,0:T(8,128)S(1)}, u32[]{:S(2)}, u32[]{:S(2)}) collective-permute-start(f32[192,256]{1,0:T(8,128)S(1)} %convolution_bitcast_fusion.11), channel_id=1, source_target_pairs={{0,16},{4,20},{8,24},{12,28},{16,0},{20,4},{24,8},{28,12},{32,48},... | collective-permute-start | bytes 589832 | tf_op jit(solution)/shard_map/ppermute | solution.py:17
  39.1 8.6 %collective-permute-done.4 = f32[192,256]{1,0:T(8,128)S(1)} collective-permute-done((f32[192,256]{1,0:T(8,128)S(1)}, f32[192,256]{1,0:T(8,128)S(1)}, u32[]{:S(2)}, u32[]{:S(2)}) %collective-permute-start.4) | collective-permute-done | bytes 196640 | tf_op jit(solution)/shard_map/ppermute | solution.py:17
  47.7 1.5 convolution_bitcast_fusion.10
  49.3 6.5 %collective-permute-start.5 = (f32[192,256]{1,0:T(8,128)S(1)}, f32[192,256]{1,0:T(8,128)S(1)}, u32[]{:S(2)}, u32[]{:S(2)}) collective-permute-start(f32[192,256]{1,0:T(8,128)S(1)} %convolution_bitcast_fusion.10), channel_id=1, source_target_pairs={{0,32},{4,36},{8,40},{12,44},{16,48},{20,52},{24,56},{28,60},{32,0... | collective-permute-start | bytes 589832 | tf_op jit(solution)/shard_map/ppermute | solution.py:17
  55.8 7.2 %collective-permute-done.5 = f32[192,256]{1,0:T(8,128)S(1)} collective-permute-done((f32[192,256]{1,0:T(8,128)S(1)}, f32[192,256]{1,0:T(8,128)S(1)}, u32[]{:S(2)}, u32[]{:S(2)}) %collective-permute-start.5) | collective-permute-done | bytes 196640 | tf_op jit(solution)/shard_map/ppermute | solution.py:17
  63.1 1.6 %convolution_bitcast_fusion.9 = f32[192,256]{1,0:T(8,128)S(1)} fusion(f32[192,256]{1,0:T(8,128)S(1)} %add.74, f32[1,6,192,192]{3,2,1,0:T(8,128)} %param.14), kind=kOutput, calls=%fused_computation.26 | convolution fusion | flops 113246208 | bytes 589824 | tf_op jit(solution)/shard_map/mk,mr->kr/dot_general | solution.py:31
  64.7 1.3 collective-permute-start.6
  66.0 3.6 %collective-permute-done.6 = f32[192,256]{1,0:T(8,128)S(1)} collective-permute-done((f32[192,256]{1,0:T(8,128)S(1)}, f32[192,256]{1,0:T(8,128)S(1)}, u32[]{:S(2)}, u32[]{:S(2)}) %collective-permute-start.6) | collective-permute-done | bytes 196640 | tf_op jit(solution)/shard_map/ppermute | solution.py:17
  69.7 1.5 convolution_bitcast_fusion.8
  71.2 2.8 %collective-permute-start.7 = (f32[192,256]{1,0:T(8,128)S(1)}, f32[192,256]{1,0:T(8,128)S(1)}, u32[]{:S(2)}, u32[]{:S(2)}) collective-permute-start(f32[192,256]{1,0:T(8,128)S(1)} %convolution_bitcast_fusion.8), channel_id=1, source_target_pairs={{0,128},{4,132},{8,136},{12,140},{16,144},{20,148},{24,152},{28,15... | collective-permute-start | bytes 589832 | tf_op jit(solution)/shard_map/ppermute | solution.py:17
  74.0 3.3 %collective-permute-done.7 = f32[192,256]{1,0:T(8,128)S(1)} collective-permute-done((f32[192,256]{1,0:T(8,128)S(1)}, f32[192,256]{1,0:T(8,128)S(1)}, u32[]{:S(2)}, u32[]{:S(2)}) %collective-permute-start.7) | collective-permute-done | bytes 196640 | tf_op jit(solution)/shard_map/ppermute | solution.py:17
  77.3 0.3 fusion.52
  77.7 0.3 fusion.23
  78.0 0.3 fusion.22
  78.4 0.3 fusion.21
  78.7 0.3 fusion.20
  79.1 0.3 fusion.19
  79.4 0.3 fusion.25
  79.7 0.3 convolution_bitcast_fusion.1
  80.1 0.1 copy-done.2
  80.2 0.4 fusion.12
  80.6 0.1 fusion.70
  80.7 0.4 copy.61
  81.1 3.8 %collective-permute-start.8 = (f32[1,375,256]{2,0,1:T(1,128)S(1)}, f32[1,375,256]{2,0,1:T(1,128)S(1)}, u32[]{:S(2)}, u32[]{:S(2)}) collective-permute-start(f32[1,375,256]{2,0,1:T(1,128)S(1)} %bitcast.158), channel_id=1, source_target_pairs={{0,4},{4,8},{8,12},{12,16},{16,20},{20,24},{24,28},{28,32},{32,36}... | collective-permute-start | bytes 1152008 | tf_op jit(solution)/shard_map/ppermute | solution.py:23
  84.9 4.6 %collective-permute-done.8 = f32[1,375,256]{2,0,1:T(1,128)S(1)} collective-permute-done((f32[1,375,256]{2,0,1:T(1,128)S(1)}, f32[1,375,256]{2,0,1:T(1,128)S(1)}, u32[]{:S(2)}, u32[]{:S(2)}) %collective-permute-start.8) | collective-permute-done | bytes 384032 | tf_op jit(solution)/shard_map/ppermute | solution.py:23
  89.5 0.5 fusion.36
  90.0 2.1 %collective-permute-start.9 = (f32[1,375,256]{2,0,1:T(1,128)S(1)}, f32[1,375,256]{2,0,1:T(1,128)S(1)}, u32[]{:S(2)}, u32[]{:S(2)}) collective-permute-start(f32[1,375,256]{2,0,1:T(1,128)S(1)} %fusion.36), channel_id=1, source_target_pairs={{4,0},{8,4},{12,8},{16,12},{20,16},{24,20},{28,24},{32,28},{36,32}... | collective-permute-start | bytes 1152008 | tf_op jit(solution)/shard_map/ppermute | solution.py:23
  92.2 7.6 %collective-permute-done.9 = f32[1,375,256]{2,0,1:T(1,128)S(1)} collective-permute-done((f32[1,375,256]{2,0,1:T(1,128)S(1)}, f32[1,375,256]{2,0,1:T(1,128)S(1)}, u32[]{:S(2)}, u32[]{:S(2)}) %collective-permute-start.9) | collective-permute-done | bytes 384032 | tf_op jit(solution)/shard_map/ppermute | solution.py:23
  99.8 0.5 fusion.35
  100.3 0.7 fusion.39
  101.0 0.8 copy.30
  101.8 0.1 reshape.96
  101.9 32.0 %all-gather.2.cloned.1.call-done = bf16[1,8,375,256]{3,2,0,1:T(8,128)(2,1)} async-done(((bf16[1,2,375,256]{3,2,0,1:T(8,128)(2,1)}), bf16[1,8,375,256]{3,2,0,1:T(8,128)(2,1)}) %all-gather.2.cloned.1.call-update) | async-done | bytes 1536016 | tf_op jit(solution)/shard_map/all_gather | solution.py:64
  133.9 5.0 %gather_fusion = bf16[32,375,256]{2,1,0:T(8,128)(2,1)} fusion(bf16[8,375,256]{2,1,0:T(8,128)(2,1)} %bitcast.154, s32[1024]{0:T(1024)S(1)} %pad_clamp_fusion), kind=kCustom, calls=%fused_computation | custom fusion | bytes 12288128 | tf_op jit(solution)/shard_map/jit(_take)/gather | solution.py:65
  138.9 11.0 %fusion.28 = f32[2,256,375]{1,2,0:T(8,128)S(1)} fusion(bf16[2,375,375]{2,0,1:T(2,128)(2,1)S(1)} %bitcast.160, bf16[2,16,375,375]{3,1,2,0:T(8,128)(2,1)} %bitcast.159, bf16[2,16,375,256]{3,2,1,0:T(8,128)(2,1)} %bitcast.155, pred[2,16]{1,0:T(4,128)(4,1)S(1)} %compare_and_fusion), kind=kOutput, calls=%fused_computation.41 | convolution fusion | flops 2451264000 | bytes 16474532 | tf_op jit(solution)/shard_map/jab,jbr->jar/dot_general | solution.py:67
  150.0 1.8 %fusion.27 = f32[1,2,375,256]{3,1,2,0:T(2,128)} fusion(f32[2,256,375]{1,2,0:T(8,128)S(1)} %fusion.28, pred[2]{0:T(512)(128)(4,1)S(1)} %get-tuple-element.6, f32[1,1,375,256]{3,1,2,0:T(1,128)S(1)} %fusion.35, f32[1,1,375,256]{3,1,2,0:T(1,128)S(1)} %bitcast.157), kind=kLoop, calls=%fused_computation.38 | loop fusion | flops 576000 | bytes 2304002 | tf_op jit(solution)/shard_map/broadcast_in_dim | solution.py:74
  (26 shorter events, 0.3 us)
Async XLA Ops:
  6.5 73.5 %copy-start = (bf16[1,2,375,375]{3,1,2,0:T(2,128)(2,1)S(1)}, bf16[1,2,375,375]{3,1,2,0:T(2,128)(2,1)}, u32[]{:S(2)}) copy-start(bf16[1,2,375,375]{3,1,2,0:T(2,128)(2,1)} %param.11) | copy-start | bytes 1687504
  6.5 127.4 %all-gather.2.cloned.1.call-start = ((), (), s32[]{:S(2)}) async-start(), calls=%async_computation | async-start | bytes 1925120 | tf_op jit(solution)/shard_map/all_gather | solution.py:64
  8.1 5.7 %collective-permute-start = (f32[192,256]{1,0:T(8,128)S(1)}, f32[192,256]{1,0:T(8,128)S(1)}, u32[]{:S(2)}, u32[]{:S(2)}) collective-permute-start(f32[192,256]{1,0:T(8,128)S(1)} %convolution_bitcast_fusion.14), channel_id=1, source_target_pairs={{0,1},{1,0},{2,3},{3,2},{4,5},{5,4},{6,7},{7,6},{8,9},{9,8},{10,11... | collective-permute-start | bytes 589832 | tf_op jit(solution)/shard_map/ppermute | solution.py:11
  13.8 7.1 %collective-permute-start.1 = (f32[192,256]{1,0:T(8,128)S(1)}, f32[192,256]{1,0:T(8,128)S(1)}, u32[]{:S(2)}, u32[]{:S(2)}) collective-permute-start(f32[192,256]{1,0:T(8,128)S(1)} %add.69), channel_id=1, source_target_pairs={{0,2},{1,3},{2,0},{3,1},{4,6},{5,7},{6,4},{7,5},{8,10},{9,11},{10,... | collective-permute-start | bytes 589832 | tf_op jit(solution)/shard_map/ppermute | solution.py:11
  22.4 4.6 %collective-permute-start.2 = (f32[192,256]{1,0:T(8,128)S(1)}, f32[192,256]{1,0:T(8,128)S(1)}, u32[]{:S(2)}, u32[]{:S(2)}) collective-permute-start(f32[192,256]{1,0:T(8,128)S(1)} %convolution_bitcast_fusion.13), channel_id=1, source_target_pairs={{0,4},{4,0},{8,12},{12,8},{16,20},{20,16},{24,28},{28,24},{32,36},... | collective-permute-start | bytes 589832 | tf_op jit(solution)/shard_map/ppermute | solution.py:17
  28.6 6.2 %collective-permute-start.3 = (f32[192,256]{1,0:T(8,128)S(1)}, f32[192,256]{1,0:T(8,128)S(1)}, u32[]{:S(2)}, u32[]{:S(2)}) collective-permute-start(f32[192,256]{1,0:T(8,128)S(1)} %convolution_bitcast_fusion.12), channel_id=1, source_target_pairs={{0,8},{4,12},{8,0},{12,4},{16,24},{20,28},{24,16},{28,20},{32,40},... | collective-permute-start | bytes 589832 | tf_op jit(solution)/shard_map/ppermute | solution.py:17
  36.3 11.4 %collective-permute-start.4 = (f32[192,256]{1,0:T(8,128)S(1)}, f32[192,256]{1,0:T(8,128)S(1)}, u32[]{:S(2)}, u32[]{:S(2)}) collective-permute-start(f32[192,256]{1,0:T(8,128)S(1)} %convolution_bitcast_fusion.11), channel_id=1, source_target_pairs={{0,16},{4,20},{8,24},{12,28},{16,0},{20,4},{24,8},{28,12},{32,48},... | collective-permute-start | bytes 589832 | tf_op jit(solution)/shard_map/ppermute | solution.py:17
  49.3 28.1 %copy-start.4 = (f32[192,192]{1,0:T(8,128)S(1)}, f32[192,192]{1,0:T(8,128)}, u32[]{:S(2)}) copy-start(f32[192,192]{1,0:T(8,128)} %param.15) | copy-start | bytes 442372
  49.3 13.8 %collective-permute-start.5 = (f32[192,256]{1,0:T(8,128)S(1)}, f32[192,256]{1,0:T(8,128)S(1)}, u32[]{:S(2)}, u32[]{:S(2)}) collective-permute-start(f32[192,256]{1,0:T(8,128)S(1)} %convolution_bitcast_fusion.10), channel_id=1, source_target_pairs={{0,32},{4,36},{8,40},{12,44},{16,48},{20,52},{24,56},{28,60},{32,0... | collective-permute-start | bytes 589832 | tf_op jit(solution)/shard_map/ppermute | solution.py:17
  63.1 14.6 %copy-start.1 = (f32[1,6,192,192]{3,2,1,0:T(8,128)S(1)}, f32[1,6,192,192]{3,2,1,0:T(8,128)}, u32[]{:S(2)}) copy-start(f32[1,6,192,192]{3,2,1,0:T(8,128)} %param.14) | copy-start | bytes 2654212
  64.7 5.0 %collective-permute-start.6 = (f32[192,256]{1,0:T(8,128)S(1)}, f32[192,256]{1,0:T(8,128)S(1)}, u32[]{:S(2)}, u32[]{:S(2)}) collective-permute-start(f32[192,256]{1,0:T(8,128)S(1)} %convolution_bitcast_fusion.9), channel_id=1, source_target_pairs={{0,64},{4,68},{8,72},{12,76},{16,80},{20,84},{24,88},{28,92},{32,9... | collective-permute-start | bytes 589832 | tf_op jit(solution)/shard_map/ppermute | solution.py:17
  71.2 6.1 %collective-permute-start.7 = (f32[192,256]{1,0:T(8,128)S(1)}, f32[192,256]{1,0:T(8,128)S(1)}, u32[]{:S(2)}, u32[]{:S(2)}) collective-permute-start(f32[192,256]{1,0:T(8,128)S(1)} %convolution_bitcast_fusion.8), channel_id=1, source_target_pairs={{0,128},{4,132},{8,136},{12,140},{16,144},{20,148},{24,152},{28,15... | collective-permute-start | bytes 589832 | tf_op jit(solution)/shard_map/ppermute | solution.py:17
  78.7 1.0 copy-start.3
  79.0 1.1 copy-start.2
  81.1 8.4 %collective-permute-start.8 = (f32[1,375,256]{2,0,1:T(1,128)S(1)}, f32[1,375,256]{2,0,1:T(1,128)S(1)}, u32[]{:S(2)}, u32[]{:S(2)}) collective-permute-start(f32[1,375,256]{2,0,1:T(1,128)S(1)} %bitcast.158), channel_id=1, source_target_pairs={{0,4},{4,8},{8,12},{12,16},{16,20},{20,24},{24,28},{28,32},{32,36}... | collective-permute-start | bytes 1152008 | tf_op jit(solution)/shard_map/ppermute | solution.py:23
  90.0 9.7 %collective-permute-start.9 = (f32[1,375,256]{2,0,1:T(1,128)S(1)}, f32[1,375,256]{2,0,1:T(1,128)S(1)}, u32[]{:S(2)}, u32[]{:S(2)}) collective-permute-start(f32[1,375,256]{2,0,1:T(1,128)S(1)} %fusion.36), channel_id=1, source_target_pairs={{4,0},{8,4},{12,8},{16,12},{20,16},{24,20},{28,24},{32,28},{36,32}... | collective-permute-start | bytes 1152008 | tf_op jit(solution)/shard_map/ppermute | solution.py:23
  100.3 1.5 copy-start.5
  133.9 5.0 %copy-start.6 = (bf16[1,2,375,375]{3,1,2,0:T(2,128)(2,1)S(1)}, bf16[1,2,375,375]{3,1,2,0:T(2,128)(2,1)}, u32[]{:S(2)}) copy-start(bf16[1,2,375,375]{3,1,2,0:T(2,128)(2,1)} %param.12) | copy-start | bytes 1687504
Sparse Core Ops, SparseCore 0:
  101.9 31.9 all-gather.1
